TPU v7x, 128 devices: a whole 4x4x4 slice. The times are simulated.
128 devices in a mesh: wide: 32 (over x, z, core), narrow: 4 (over y).
Axes of the slice: x: 4, y: 4, z: 4, core: 2. Of those that a mesh axis runs over, the one named last changes fastest.
Arguments:
- tokens: bfloat16 [262144, 1024], P(('wide', 'narrow')), may hold values from -64 to 64
- slot_params: bfloat16 [1024, 512], replicated, may hold values from -2.5 to 2.5
- expert_in: bfloat16 [128, 1024, 4096], P('wide', None, 'narrow'), may hold values from -0.1875 to 0.1875
- expert_out: bfloat16 [128, 4096, 1024], P('wide', 'narrow'), may hold values from -0.09375 to 0.09375
Outputs:
- mixed: bfloat16 [262144, 1024], P(('wide', 'narrow'))
All inputs are finite; a program needn't handle non-finite values.
Results may differ from a plain program's by a relative error of at most 0.0071.
Values may be sent and summed in bfloat16 or wider, within the bound.
A program may use at most 128 MiB of HBM per device.

v0:
```python
import jax
import jax.numpy as jnp
from jax import lax
from jax.sharding import PartitionSpec as P

SLOT_PER = 4


def divide_rows(summed, slot_totals):
    return (summed / slot_totals[:, None]).astype(jnp.bfloat16)


def shards(tokens, slot_params, expert_in, expert_out):
    logits = jnp.dot(tokens, slot_params, preferred_element_type=jnp.float32)
    local_peak = jnp.max(logits, axis=0)
    column_peak = lax.pmax(local_peak, ("wide", "narrow"))
    weights = jnp.exp(logits - column_peak)
    slot_totals = lax.psum(jnp.sum(weights, axis=0), ("wide", "narrow"))
    dispatch = weights.astype(jnp.bfloat16)
    slot_count = slot_params.shape[1]
    row_count = slot_count // lax.axis_size("wide")
    columns = dispatch
    partial_value = lax.psum_scatter(
        lax.dot_general(
            columns, tokens, (((0,), (0,)), ((), ())), preferred_element_type=jnp.float32
        ),
        "wide",
        scatter_dimension=0,
        tiled=True,
    )
    summed = lax.psum(partial_value, "narrow")
    owned_totals = lax.dynamic_slice_in_dim(
        slot_totals, lax.axis_index("wide") * row_count, row_count
    )
    slot_in = divide_rows(summed, owned_totals)
    slot_stack = slot_in.reshape(expert_in.shape[0], SLOT_PER, slot_in.shape[1])
    hidden = jax.nn.gelu(
        jnp.einsum("esd,edh->esh", slot_stack, expert_in, preferred_element_type=jnp.float32)
    ).astype(jnp.bfloat16)
    expert_sum = jnp.einsum("esh,ehd->esd", hidden, expert_out, preferred_element_type=jnp.float32)
    expert_sum = expert_sum.reshape(-1, expert_sum.shape[2])
    mixing = jax.nn.softmax(logits, axis=1).astype(jnp.bfloat16)
    whole_rows = lax.psum(expert_sum, "narrow").astype(jnp.bfloat16)
    columns = mixing
    mixed = jnp.dot(
        columns,
        lax.all_gather(whole_rows, "wide", axis=0, tiled=True),
        preferred_element_type=jnp.float32,
    )
    return mixed.astype(jnp.bfloat16)


def solution(mesh):
    return jax.shard_map(
        shards,
        mesh=mesh,
        in_specs=(
            P(("wide", "narrow"), None),
            P(),
            P("wide", None, "narrow"),
            P("wide", "narrow", None),
        ),
        out_specs=P(("wide", "narrow"), None),
        check_vma=False,
    )
```

profile of v0, /device:TPU:1, one launch (start us, length us, event | category | flops | bytes accessed | tf_op | source)
XLA Modules:
  0.0 312.3 jit_solution(13459068889585292751)
XLA Ops:
  6.5 0.0 copy-start
  6.5 0.0 reduce-scatter.2.cloned.1.call-start
  6.5 1.2 copy-done
  7.8 6.5 %fusion.26 = (f32[2048]{0:T(1024)S(1)}, f32[512]{0:T(512)S(1)}, f32[2048,512]{1,0:T(8,128)}) fusion(bf16[2048,1024]{1,0:T(8,128)(2,1)} %param.4, bf16[1024,512]{1,0:T(8,128)(2,1)S(1)} %copy-done), kind=kOutput, calls=%fused_computation.30 | convolution fusion | flops 2149578240 | bytes 9447424 | tf_op jit(solution)/shard_map/dot_general | solution.py:14
  14.2 68.6 %pmax.7 = f32[512]{0:T(512)S(1)} all-reduce(f32[512]{0:T(512)S(1)} %get-tuple-element.8), channel_id=1, replica_groups=mesh['wide'=32,'narrow'=4] {'wide','narrow'}, use_global_device_ids=true, to_apply=%region_3.0 | all-reduce | flops 512 | bytes 4096 | tf_op jit(solution)/shard_map/pmax | solution.py:16
  82.8 7.2 %fusion.3 = f32[512,1024]{1,0:T(8,128)} fusion(bf16[2048,1024]{1,0:T(8,128)(2,1)} %param.4, f32[2048,512]{1,0:T(8,128)} %get-tuple-element.9, f32[512]{0:T(512)S(1)} %pmax.7), kind=kOutput, calls=%fused_computation.7 | convolution fusion | flops 2149580800 | bytes 10487808 | tf_op jit(solution)/shard_map/dot_general | solution.py:24
  90.0 0.0 reduce-scatter.2.cloned.1.call-update
  90.0 0.0 all-reduce.2.cloned.1.call-start
  90.1 73.9 %reduce-scatter.2.cloned.1.call-done = f32[16,1024]{1,0:T(8,128)} async-done(((f32[512,1024]{1,0:T(8,128)}), f32[16,1024]{1,0:T(8,128)}) %reduce-scatter.2.cloned.1.call-update) | async-done | bytes 65552 | tf_op jit(solution)/shard_map/reduce_scatter | solution.py:23
  163.9 0.0 all-reduce.2.cloned.1.call-update
  164.0 0.0 all-gather.2.cloned.1.call-start
  164.0 3.1 %fusion = (f32[2048]{0:T(1024)S(1)}, f32[512]{0:T(512)S(1)}) fusion(f32[2048,512]{1,0:T(8,128)} %get-tuple-element.9, f32[2048]{0:T(1024)S(1)} %get-tuple-element.7, f32[512]{0:T(512)S(1)} %pmax.7), kind=kLoop, calls=%fused_computation.4 | loop fusion | flops 4191744 | bytes 4214784 | tf_op jit(solution)/shard_map/reduce_sum | solution.py:42
  167.2 66.0 %psum.22 = f32[512]{0:T(512)S(1)} all-reduce(f32[512]{0:T(512)S(1)} %get-tuple-element.6), channel_id=1, replica_groups=mesh['wide'=32,'narrow'=4] {'wide','narrow'}, use_global_device_ids=true, to_apply=%region_7.0 | all-reduce | flops 512 | bytes 4096 | tf_op jit(solution)/shard_map/psum | solution.py:18
  233.2 0.1 dynamic_slice.3
  233.3 0.0 all-reduce.2.cloned.1.call-done
  233.3 0.9 divide_convert_fusion.2
  234.2 8.0 %fusion.16 = f32[4,4,1024]{2,1,0:T(4,128)S(1)} fusion(bf16[4,1024,1024]{2,1,0:T(8,128)(2,1)} %param.7, bf16[4,4,1024]{2,1,0:T(4,128)(2,1)S(1)} %reshape.10, bf16[4,1024,1024]{2,1,0:T(8,128)(2,1)} %param.6), kind=kOutput, calls=%fused_computation.21 | convolution fusion | flops 67256320 | bytes 16875520 | tf_op jit(solution)/shard_map/esh,ehd->esd/dot_general | solution.py:40
  242.3 12.6 %psum.23 = bf16[16,1024]{1,0:T(8,128)(2,1)} all-reduce(f32[16,1024]{1,0:T(8,128)S(1)} %reshape.11), channel_id=1, replica_groups=mesh['wide'=32,'narrow'=4] {'narrow'}, use_global_device_ids=true, to_apply=%region_8.0 | all-reduce | flops 16384 | bytes 98304 | tf_op jit(solution)/shard_map/psum | solution.py:43
  254.9 0.0 all-gather.2.cloned.1.call-update
  254.9 43.9 %all-gather.2.cloned.1.call-done = bf16[512,1024]{1,0:T(8,128)(2,1)} async-done(((bf16[16,1024]{1,0:T(8,128)(2,1)}), bf16[512,1024]{1,0:T(8,128)(2,1)}) %all-gather.2.cloned.1.call-update) | async-done | bytes 1048592 | tf_op jit(solution)/shard_map/all_gather | solution.py:47
  298.7 7.0 %convolution_convert_fusion = bf16[2048,1024]{1,0:T(8,128)(2,1)} fusion(bf16[512,1024]{1,0:T(8,128)(2,1)} %all-gather.2.cloned.1.call-done, f32[2048,512]{1,0:T(8,128)} %get-tuple-element.9, f32[2048]{0:T(1024)S(1)} %get-tuple-element.5, f32[2048]{0:T(1024)S(1)} %get-tuple-element.7), kind=kOutput, calls=%fused_computation.3 | convolution fusion | flops 2152726528 | bytes 9453568 | tf_op jit(solution)/shard_map/dot_general | solution.py:45
  (2 shorter events, 0.1 us)
Async XLA Ops:
  6.5 1.2 copy-start
  6.5 157.4 %reduce-scatter.2.cloned.1.call-start = ((), (), s32[]{:S(2)}) async-start(), calls=%async_computation.1 | async-start | bytes 2162688 | tf_op jit(solution)/shard_map/reduce_scatter | solution.py:23
  90.0 143.2 %all-reduce.2.cloned.1.call-start = ((), (), s32[]{:S(2)}) async-start(), calls=%async_computation.2 | async-start | bytes 131072 | tf_op jit(solution)/shard_map/psum | solution.py:31
  164.0 134.8 %all-gather.2.cloned.1.call-start = ((), (), s32[]{:S(2)}) async-start(), calls=%async_computation.3 | async-start | bytes 1081344 | tf_op jit(solution)/shard_map/all_gather | solution.py:47
Sparse Core Ops, SparseCore 0:
  90.2 73.7 reduce-scatter.1
  166.2 40.1 all-reduce.1
  255.0 43.6 all-gather.1
where the time goes:
time: 313 us; the launch traced here: 312 us
  blocking collectives  147 us (47%)
  waiting for transfers between devices  118 us (38%)
  matrix products  28.7 us (9%)
  between operations  13.1 us (4%)
  other arithmetic  4.06 us (1%)
    reduce_scatter x1, waiting for transfers between devices, shards(): lax.psum_scatter(lax.dot_general(columns, tokens, (((0,), (0,)), ((), ())...  73.9 us
    pmax x1, blocking collectives, shards(): column_peak = lax.pmax(local_peak, ('wide', 'narrow'))  68.6 us
    psum x1, blocking collectives, shards(): slot_totals = lax.psum(jnp.sum(weights, axis=0), ('wide', 'narrow'))  66 us
    all_gather x1, waiting for transfers between devices, shards(): lax.all_gather(whole_rows, 'wide', axis=0, tiled=True)  43.9 us
    psum x1, blocking collectives, shards(): whole_rows = lax.psum(expert_sum, 'narrow').astype(jnp.bfloat16)  12.6 us
    dot_general x1, matrix products, shards(): jnp.einsum('esh,ehd->esd', hidden, expert_out, preferred_element_type=jnp...  8.04 us
    dot_general x1, matrix products, shards(): lax.dot_general(columns, tokens, (((0,), (0,)), ((), ())), preferred_elem...  7.15 us
    dot_general x1, matrix products, shards(): jnp.dot(columns, lax.all_gather(whole_rows, 'wide', axis=0, tiled=True),...  7.05 us
  transfers between devices with their start and end apart: 3, of which 2 were waited for; matrix products, arithmetic and copies ran while one was open for 1% of the time, Pallas kernels for 0%

commit v1 on v0

--- a/solution.py
+++ b/solution.py
@@ -4,6 +4,18 @@
 from jax.sharding import PartitionSpec as P
 
 SLOT_PER = 4
+
+
+def collect(x, axis, dim):
+    ways, here = (lax.axis_size(axis), lax.axis_index(axis))
+    grown, reach = (x, 1)
+    while reach < ways:
+        theirs = lax.ppermute(grown, axis, [(d, d ^ reach) for d in range(ways)])
+        mine_first = jnp.concatenate([grown, theirs], axis=dim)
+        theirs_first = jnp.concatenate([theirs, grown], axis=dim)
+        grown = jnp.where(here & reach == 0, mine_first, theirs_first)
+        reach = 2 * reach
+    return grown
 
 
 def divide_rows(summed, slot_totals):
@@ -42,11 +54,7 @@
     mixing = jax.nn.softmax(logits, axis=1).astype(jnp.bfloat16)
     whole_rows = lax.psum(expert_sum, "narrow").astype(jnp.bfloat16)
     columns = mixing
-    mixed = jnp.dot(
-        columns,
-        lax.all_gather(whole_rows, "wide", axis=0, tiled=True),
-        preferred_element_type=jnp.float32,
-    )
+    mixed = jnp.dot(columns, collect(whole_rows, "wide", 0), preferred_element_type=jnp.float32)
     return mixed.astype(jnp.bfloat16)
 
 

time: 313 us -> 303 us (0.968)
  waiting for transfers between devices: 118 us -> 94.8 us
  starting transfers between devices: 0.08 us -> 11.5 us
    all_gather x1 -> x0, waiting for transfers between devices: 43.9 us -> none  [shards(): lax.all_gather(whole_rows, 'wide', axis=0, tiled=True)]
    ppermute x0 -> x5, waiting for transfers between devices: none -> 20.9 us  [collect(): theirs = lax.ppermute(grown, axis, [(d, d ^ reach) for d in range(ways)])]
    ppermute x0 -> x5, starting transfers between devices: none -> 11.4 us  [collect(): theirs = lax.ppermute(grown, axis, [(d, d ^ reach) for d in range(ways)])]
  transfers between devices with their start and end apart: 3 -> 7, of which waited for: 2 -> 6; matrix products, arithmetic and copies ran while one was open for 1% -> 1% of each run, Pallas kernels for 0% -> 0%
where the time goes in v1:
time: 303 us; the launch traced here: 300 us
  blocking collectives  146 us (48%)
  waiting for transfers between devices  94.8 us (31%)
  matrix products  28.4 us (9%)
  between operations  13.5 us (4%)
  starting transfers between devices  11.5 us (4%)
  other arithmetic  4.29 us (1%)
    reduce_scatter x1, waiting for transfers between devices, shards(): lax.psum_scatter(lax.dot_general(columns, tokens, (((0,), (0,)), ((), ())...  73.9 us
    pmax x1, blocking collectives, shards(): column_peak = lax.pmax(local_peak, ('wide', 'narrow'))  68.6 us
    psum x1, blocking collectives, shards(): slot_totals = lax.psum(jnp.sum(weights, axis=0), ('wide', 'narrow'))  66 us
    ppermute x5, waiting for transfers between devices, collect(): theirs = lax.ppermute(grown, axis, [(d, d ^ reach) for d in range(ways)])  20.9 us
    psum x1, blocking collectives, shards(): whole_rows = lax.psum(expert_sum, 'narrow').astype(jnp.bfloat16)  11.8 us
    ppermute x5, starting transfers between devices, collect(): theirs = lax.ppermute(grown, axis, [(d, d ^ reach) for d in range(ways)])  11.4 us
    dot_general x1, matrix products, shards(): jnp.einsum('esh,ehd->esd', hidden, expert_out, preferred_element_type=jnp...  8.04 us
    dot_general x1, matrix products, shards(): lax.dot_general(columns, tokens, (((0,), (0,)), ((), ())), preferred_elem...  7.15 us
  transfers between devices with their start and end apart: 7, of which 6 were waited for; matrix products, arithmetic and copies ran while one was open for 1% of the time, Pallas kernels for 0%

profile of v1, /device:TPU:1, one launch (start us, length us, event | category | flops | bytes accessed | tf_op | source)
XLA Modules:
  0.0 300.2 jit_solution(7513175797798102541)
XLA Ops:
  6.5 0.0 copy-start
  6.5 0.0 reduce-scatter.2.cloned.1.call-start
  6.5 1.2 copy-done
  7.8 6.5 %fusion.33 = (f32[512]{0:T(512)S(1)}, f32[2048]{0:T(1024)S(1)}, f32[2048,512]{1,0:T(8,128)}) fusion(bf16[2048,1024]{1,0:T(8,128)(2,1)} %param.4, bf16[1024,512]{1,0:T(8,128)(2,1)S(1)} %copy-done), kind=kOutput, calls=%fused_computation.42 | convolution fusion | flops 2149578240 | bytes 9447424 | tf_op jit(solution)/shard_map/dot_general | solution.py:26
  14.2 68.6 %pmax.7 = f32[512]{0:T(512)S(1)} all-reduce(f32[512]{0:T(512)S(1)} %get-tuple-element.7), channel_id=1, replica_groups=mesh['wide'=32,'narrow'=4] {'wide','narrow'}, use_global_device_ids=true, to_apply=%region_3.0 | all-reduce | flops 512 | bytes 4096 | tf_op jit(solution)/shard_map/pmax | solution.py:28
  82.9 7.2 %fusion.3 = f32[512,1024]{1,0:T(8,128)} fusion(bf16[2048,1024]{1,0:T(8,128)(2,1)} %param.4, f32[2048,512]{1,0:T(8,128)} %get-tuple-element.9, f32[512]{0:T(512)S(1)} %pmax.7), kind=kOutput, calls=%fused_computation.7 | convolution fusion | flops 2149580800 | bytes 10487808 | tf_op jit(solution)/shard_map/dot_general | solution.py:36
  90.0 0.0 reduce-scatter.2.cloned.1.call-update
  90.0 0.0 all-reduce.2.cloned.1.call-start
  90.1 73.9 %reduce-scatter.2.cloned.1.call-done = f32[16,1024]{1,0:T(8,128)} async-done(((f32[512,1024]{1,0:T(8,128)}), f32[16,1024]{1,0:T(8,128)}) %reduce-scatter.2.cloned.1.call-update) | async-done | bytes 65552 | tf_op jit(solution)/shard_map/reduce_scatter | solution.py:35
  164.0 0.0 all-reduce.2.cloned.1.call-update
  164.0 3.2 %fusion.1 = (f32[512]{0:T(512)S(1)}, f32[2048]{0:T(1024)S(1)}) fusion(f32[2048,512]{1,0:T(8,128)} %get-tuple-element.9, f32[512]{0:T(512)S(1)} %pmax.7, f32[2048]{0:T(1024)S(1)} %get-tuple-element.8), kind=kLoop, calls=%fused_computation.5 | loop fusion | flops 4191744 | bytes 4214784 | tf_op jit(solution)/shard_map/reduce_sum | solution.py:30
  167.2 66.0 %psum.22 = f32[512]{0:T(512)S(1)} all-reduce(f32[512]{0:T(512)S(1)} %get-tuple-element.5), channel_id=1, replica_groups=mesh['wide'=32,'narrow'=4] {'wide','narrow'}, use_global_device_ids=true, to_apply=%region_7.0 | all-reduce | flops 512 | bytes 4096 | tf_op jit(solution)/shard_map/psum | solution.py:30
  233.2 0.1 dynamic_slice.3
  233.2 0.0 all-reduce.2.cloned.1.call-done
  233.2 0.9 divide_convert_fusion.2
  234.2 8.0 %fusion.22 = f32[4,4,1024]{2,1,0:T(4,128)S(1)} fusion(bf16[4,1024,1024]{2,1,0:T(8,128)(2,1)} %param.7, bf16[4,4,1024]{2,1,0:T(4,128)(2,1)S(1)} %reshape.10, bf16[4,1024,1024]{2,1,0:T(8,128)(2,1)} %param.6), kind=kOutput, calls=%fused_computation.32 | convolution fusion | flops 67256320 | bytes 16875520 | tf_op jit(solution)/shard_map/esh,ehd->esd/dot_general | solution.py:52
  242.3 11.8 %psum.23 = bf16[16,1024]{1,0:T(8,128)(2,1)S(1)} all-reduce(f32[16,1024]{1,0:T(8,128)S(1)} %reshape.11), channel_id=1, replica_groups=mesh['wide'=32,'narrow'=4] {'narrow'}, use_global_device_ids=true, to_apply=%region_8.0 | all-reduce | flops 16384 | bytes 98304 | tf_op jit(solution)/shard_map/psum | solution.py:55
  254.0 4.5 %collective-permute-start = (bf16[16,1024]{1,0:T(8,128)(2,1)S(1)}, bf16[16,1024]{1,0:T(8,128)(2,1)S(1)}, u32[]{:S(2)}, u32[]{:S(2)}) collective-permute-start(bf16[16,1024]{1,0:T(8,128)(2,1)S(1)} %psum.23), channel_id=1, source_target_pairs={{0,4},{4,0},{8,12},{12,8},{16,20},{20,16},{24,28},{28,24},{32,36},... | collective-permute-start | bytes 98312 | tf_op jit(solution)/shard_map/ppermute | solution.py:13
  258.5 0.9 collective-permute-done
  259.3 1.3 collective-permute-start.1
  260.6 1.9 collective-permute-done.1
  262.6 2.3 collective-permute-start.2
  264.9 3.1 %collective-permute-done.2 = bf16[64,1024]{1,0:T(8,128)(2,1)S(1)} collective-permute-done((bf16[64,1024]{1,0:T(8,128)(2,1)S(1)}, bf16[64,1024]{1,0:T(8,128)(2,1)S(1)}, u32[]{:S(2)}, u32[]{:S(2)}) %collective-permute-start.2) | collective-permute-done | bytes 131104 | tf_op jit(solution)/shard_map/ppermute | solution.py:13
  268.0 1.3 collective-permute-start.3
  269.3 4.0 %collective-permute-done.3 = bf16[128,1024]{1,0:T(8,128)(2,1)S(1)} collective-permute-done((bf16[128,1024]{1,0:T(8,128)(2,1)S(1)}, bf16[128,1024]{1,0:T(8,128)(2,1)S(1)}, u32[]{:S(2)}, u32[]{:S(2)}) %collective-permute-start.3) | collective-permute-done | bytes 262176 | tf_op jit(solution)/shard_map/ppermute | solution.py:13
  273.3 0.1 maximum_select_fusion.2
  273.5 2.0 collective-permute-start.4
  275.5 11.1 %collective-permute-done.4 = bf16[256,1024]{1,0:T(8,128)(2,1)S(1)} collective-permute-done((bf16[256,1024]{1,0:T(8,128)(2,1)S(1)}, bf16[256,1024]{1,0:T(8,128)(2,1)S(1)}, u32[]{:S(2)}, u32[]{:S(2)}) %collective-permute-start.4) | collective-permute-done | bytes 524320 | tf_op jit(solution)/shard_map/ppermute | solution.py:13
  286.6 6.8 %convolution_convert_fusion = bf16[2048,1024]{1,0:T(8,128)(2,1)} fusion(f32[2048,512]{1,0:T(8,128)} %get-tuple-element.9, f32[2048]{0:T(1024)S(1)} %get-tuple-element.6, f32[2048]{0:T(1024)S(1)} %get-tuple-element.8, bf16[256,1024]{1,0:T(8,128)(2,1)S(1)} %collective-permute-done.4, bf16[256,1024]{1,0:T(8,128)(2,1)S(1)} %maximum_select_fusion.2, pred[]{:T(512)S(6)} %eq.15), kind=kOutput, calls=%fused_computation.3 | convolution fusion | flops 2157445120 | bytes 9453569 | tf_op jit(solution)/shard_map/dot_general | solution.py:57
  (5 shorter events, 0.1 us)
Async XLA Ops:
  6.5 1.2 copy-start
  6.5 157.4 %reduce-scatter.2.cloned.1.call-start = ((), (), s32[]{:S(2)}) async-start(), calls=%async_computation.1 | async-start | bytes 2162688 | tf_op jit(solution)/shard_map/reduce_scatter | solution.py:35
  90.0 143.2 %all-reduce.2.cloned.1.call-start = ((), (), s32[]{:S(2)}) async-start(), calls=%async_computation.2 | async-start | bytes 131072 | tf_op jit(solution)/shard_map/psum | solution.py:43
  254.0 5.3 %collective-permute-start = (bf16[16,1024]{1,0:T(8,128)(2,1)S(1)}, bf16[16,1024]{1,0:T(8,128)(2,1)S(1)}, u32[]{:S(2)}, u32[]{:S(2)}) collective-permute-start(bf16[16,1024]{1,0:T(8,128)(2,1)S(1)} %psum.23), channel_id=1, source_target_pairs={{0,4},{4,0},{8,12},{12,8},{16,20},{20,16},{24,28},{28,24},{32,36},... | collective-permute-start | bytes 98312 | tf_op jit(solution)/shard_map/ppermute | solution.py:13
  259.3 3.2 %collective-permute-start.1 = (bf16[32,1024]{1,0:T(8,128)(2,1)S(1)}, bf16[32,1024]{1,0:T(8,128)(2,1)S(1)}, u32[]{:S(2)}, u32[]{:S(2)}) collective-permute-start(bf16[32,1024]{1,0:T(8,128)(2,1)S(1)} %maximum_select_fusion.5), channel_id=1, source_target_pairs={{0,8},{4,12},{8,0},{12,4},{16,24},{20,28},{24,16},{28,20},{32,40},... | collective-permute-start | bytes 196616 | tf_op jit(solution)/shard_map/ppermute | solution.py:13
  262.6 5.4 %collective-permute-start.2 = (bf16[64,1024]{1,0:T(8,128)(2,1)S(1)}, bf16[64,1024]{1,0:T(8,128)(2,1)S(1)}, u32[]{:S(2)}, u32[]{:S(2)}) collective-permute-start(bf16[64,1024]{1,0:T(8,128)(2,1)S(1)} %maximum_select_fusion.4), channel_id=1, source_target_pairs={{0,16},{4,20},{8,24},{12,28},{16,0},{20,4},{24,8},{28,12},{32,48},... | collective-permute-start | bytes 393224 | tf_op jit(solution)/shard_map/ppermute | solution.py:13
  268.0 5.3 %collective-permute-start.3 = (bf16[128,1024]{1,0:T(8,128)(2,1)S(1)}, bf16[128,1024]{1,0:T(8,128)(2,1)S(1)}, u32[]{:S(2)}, u32[]{:S(2)}) collective-permute-start(bf16[128,1024]{1,0:T(8,128)(2,1)S(1)} %maximum_select_fusion.3), channel_id=1, source_target_pairs={{0,32},{4,36},{8,40},{12,44},{16,48},{20,52},{24,56},{28,60},{32,0... | collective-permute-start | bytes 786440 | tf_op jit(solution)/shard_map/ppermute | solution.py:13
  273.5 13.1 %collective-permute-start.4 = (bf16[256,1024]{1,0:T(8,128)(2,1)S(1)}, bf16[256,1024]{1,0:T(8,128)(2,1)S(1)}, u32[]{:S(2)}, u32[]{:S(2)}) collective-permute-start(bf16[256,1024]{1,0:T(8,128)(2,1)S(1)} %maximum_select_fusion.2), channel_id=1, source_target_pairs={{0,64},{4,68},{8,72},{12,76},{16,80},{20,84},{24,88},{28,92},{32,9... | collective-permute-start | bytes 1572872 | tf_op jit(solution)/shard_map/ppermute | solution.py:13
Sparse Core Ops, SparseCore 0:
  90.1 73.7 reduce-scatter.1
  166.3 40.0 all-reduce.1
